TPU v7x, 256 devices: a whole 4x4x8 slice. The times are simulated.
256 devices in a mesh: row: 8 (over x, core), col: 32 (over z, y).
Axes of the slice: x: 4, y: 4, z: 8, core: 2. Of those that a mesh axis runs over, the one named last changes fastest.
Arguments:
- pair_rep: bfloat16 [2048, 2048, 128], P('row', 'col'), may hold values from -6 to 6
- queries: bfloat16 [2048, 192], P(('row', 'col')), may hold values from -12 to 12
- qpoints: bfloat16 [2048, 144], P(('row', 'col')), may hold values from -6 to 6
- frames: float32 [2048, 12], P(('row', 'col')), may hold values from -4 to 4, as said below
- keyset: bfloat16 [2048, 192], P('col', 'row'), may hold values from -12 to 12
- kpoints: bfloat16 [2048, 144], P('col', 'row'), may hold values from -6 to 6
- values: bfloat16 [2048, 192], P('col', 'row'), may hold values from -6 to 6
- vpoints: bfloat16 [2048, 288], P('col', 'row'), may hold values from -6 to 6
- key_mask: int32 [2048], P('col'), may hold values 0 or 1
- bias_weight: bfloat16 [128, 12], replicated, may hold values from -0.5 to 0.5
- head_weight: float32 [12], replicated, may hold values from -1.5 to 1.5
- grad_scalar: bfloat16 [2048, 192], P(('row', 'col')), may hold values from -6 to 6
- grad_pair: bfloat16 [2048, 1536], P(('row', 'col')), may hold values from -6 to 6
- grad_points: bfloat16 [2048, 288], P(('row', 'col')), may hold values from -6 to 6
Outputs:
- pair_grad: bfloat16 [2048, 2048, 128], P('row', 'col')
- queries_grad: float32 [2048, 192], P(('row', 'col'))
- qpoints_grad: float32 [2048, 144], P(('row', 'col'))
- keyset_grad: float32 [2048, 192], P('col', 'row')
- kpoints_grad: float32 [2048, 144], P('col', 'row')
- values_grad: float32 [2048, 192], P('col', 'row')
- vpoints_grad: float32 [2048, 288], P('col', 'row')
- bias_grad: float32 [128, 12], replicated
- head_grad: float32 [12], replicated
Inputs may be any that keep to these rules, and one draw needn't show every extreme that they name: `frames`: each row is a rotation matrix, row-major, followed by a translation.
All inputs are finite; a program needn't handle non-finite values. No bound on the sum of `key_mask` on one device may be relied on, other than what follows from the above.
Results may differ from a plain program's by a relative error of at most 0.023.
Values may be sent and summed in bfloat16 or wider, within the bound.
A program may use at most 64 MiB of HBM per device.

v0:
```python
import functools
import math

import jax
import jax.numpy as jnp
from jax import lax
from jax.experimental import pallas as pl
from jax.experimental.pallas import tpu as pltpu
from jax.sharding import PartitionSpec as P

H = 12
C = 16
CZ = 128
PQ = 4
PV = 8
LANES = 128
ROWS = 8
FEATURES = 1024
MESH = pl.DeviceIdType.MESH
F32 = jnp.float32
BF16 = jnp.bfloat16
WL = math.sqrt(1.0 / 3.0)
WC = math.sqrt(2.0 / (9.0 * PQ))
DIST_WEIGHT = 0.5 * WL * WC


def nt(a, b):
    return lax.dot_general(a, b, (((1,), (1,)), ((), ())), preferred_element_type=F32)


def nn(a, b):
    return lax.dot_general(a, b, (((1,), (0,)), ((), ())), preferred_element_type=F32)


def iota(shape, dim):
    return lax.broadcasted_iota(jnp.int32, shape, dim).astype(F32)


def whole_part(x, divisor):
    return jnp.floor((x + 0.5) * (1.0 / divisor))


def padded(scratch, array, width):
    rows, used = array.shape
    scratch[0:rows, 0:width] = jnp.zeros((rows, width), F32)
    scratch[0:rows, 0:used] = array.astype(F32)
    return scratch[0:rows, 0:width]


def rotated(frames, points, width, back):
    lane = iota((ROWS, width), 1)
    place = lane - 3.0 * whole_part(lane, 3)
    total = jnp.zeros((ROWS, width), F32)
    for step in range(-2, 3):
        factor = jnp.zeros((ROWS, width), F32)
        for a in range(3):
            b = a + step
            if 0 <= b < 3:
                at = 3 * b + a if back else 3 * a + b
                factor = jnp.where(place == float(a), frames[:, at : at + 1], factor)
        moved = points if step == 0 else pltpu.roll(points, (-step) % width, 1)
        total = total + factor * moved
    return total


def shifted(frames, width):
    lane = iota((ROWS, width), 1)
    place = lane - 3.0 * whole_part(lane, 3)
    total = jnp.zeros((ROWS, width), F32)
    for a in range(3):
        total = jnp.where(place == float(a), frames[:, 9 + a : 10 + a], total)
    return jnp.where(lane < 3.0 * H * PQ, total, 0.0)


def feature_heads():
    lane = iota((1, FEATURES), 1)
    heads = whole_part(lane, C)
    points = whole_part(lane - 256.0, 3 * PQ)
    scalars = whole_part(lane - 512.0, C)
    globals_ = whole_part(lane - 704.0, 3 * PV)
    none = jnp.full((1, FEATURES), 99.0, F32)
    heads = jnp.where(lane < 192.0, heads, none)
    heads = jnp.where((lane >= 256.0) & (lane < 400.0), points, heads)
    heads = jnp.where((lane >= 512.0) & (lane < 704.0), scalars, heads)
    return jnp.where((lane >= 704.0) & (lane < 992.0), globals_, heads)


def head_mask():
    row = whole_part(iota((LANES, FEATURES), 0), ROWS)
    return jnp.where(row == feature_heads(), 1.0, 0.0)


def fill_placing(placing):
    lane = iota((LANES, 1), 0)
    for r in range(8):
        place = jnp.full((LANES, 1), -1.0, F32)
        for first, width, base in ((0, 24, 0), (24, 18, 256), (42, 24, 512), (66, 36, 704)):
            inside = (lane >= float(first)) & (lane < float(first + width))
            place = jnp.where(inside, lane + float(base + r * width - first), place)
        at = iota((LANES, FEATURES), 1)
        placing[r * LANES : (r + 1) * LANES, :] = jnp.where(at == place, 1.0, 0.0).astype(BF16)


def per_head(values, heads):
    total = jnp.zeros(heads.shape, F32)
    for h in range(H):
        total = jnp.where(heads == float(h), values[h], total)
    return total


def softplus_of(x):
    return jnp.log(1.0 + jnp.exp(x))


def lane_heads():
    return whole_part(iota((1, LANES), 1), ROWS)


def fill_weight(expanded, bias_weight):
    row = whole_part(iota((LANES, H), 0), ROWS)
    pick = jnp.where(row == iota((LANES, H), 1), 1.0, 0.0).astype(BF16)
    rows = nn(pick, bias_weight)
    residue = iota((LANES, LANES), 0)
    residue = residue - ROWS * whole_part(residue, ROWS)
    for i in range(ROWS):
        expanded[:, i * LANES : (i + 1) * LANES] = jnp.where(
            residue == float(i), rows, 0.0
        ).astype(BF16)


def residue_masks():
    row = iota((H * ROWS, LANES), 0)
    row = row - ROWS * whole_part(row, ROWS)
    return [jnp.where(row == float(i), 1.0, 0.0).astype(BF16) for i in range(ROWS)]


def expanded_pairs(block, masks):
    pairs = block[0 : H * ROWS, :]
    wide = jnp.concatenate([pairs * m for m in masks], axis=1)
    return jnp.concatenate([wide, jnp.zeros((LANES - H * ROWS, FEATURES), BF16)], axis=0)


def expanded_features(features, mask):
    twice = jnp.concatenate([features, features], axis=0).astype(BF16)
    return jnp.concatenate([twice] * ROWS, axis=0) * mask


def wide_features(block):
    tall = block[H * ROWS :, :].astype(F32)
    return jnp.concatenate([tall[t * ROWS : (t + 1) * ROWS] for t in range(ROWS)], axis=1)


def make_block(block, queries, qpoints, frames, gscalar, gpair, gpoints, wide, loss):
    f = frames[...]
    q = padded(wide, queries[...], 256)
    points = padded(wide, qpoints[...], 256)
    qg = rotated(f, points, 256, False) + shifted(f, 256)
    gs = padded(wide, gscalar[...], 256) * loss
    gg = rotated(f, padded(wide, gpoints[...], 384) * loss, 384, False)
    gg = pltpu.roll(gg, 64, 1)
    tiles = [q[:, :128], q[:, 128:], qg[:, :128], qg[:, 128:], gs[:, :128]]
    tiles += [gs[:, 128:] + gg[:, :128], gg[:, 128:256], gg[:, 256:]]
    pairs = gpair[...].astype(F32) * loss
    tall = [pairs[:, h * CZ : (h + 1) * CZ] for h in range(H)]
    block[...] = jnp.concatenate(tall + tiles, axis=0).astype(BF16)


def make_key_piece(piece, keyset, kpoints, values, vpoints, tall):
    at = 0
    tall[...] = jnp.zeros_like(tall)
    for array in (keyset, kpoints, values, vpoints):
        tall[at : at + array.shape[0], :] = array[...].astype(F32)
        at += array.shape[0]
    piece[...] = tall[...].T.astype(BF16)


def gray(i):
    return i + (i // 2) * (1 - 2 * (i % 2))


def ring_slots(e, z, y):
    s, i = (e + 2) // 4, (e + 2) % 4
    turn = s // 4 + (4 - s) // 4
    low = ((z + 8 - s) % 8) * 4 + (y + gray(i)) % 4
    high = ((z + s) % 8) * 4 + (y + gray((i + 2 * turn) % 4)) % 4
    return low, high


def near_slot(n, z, y):
    m, i = n // 4, n % 4
    dz = ((m + 1) // 2) * (2 * (m % 2) - 1)
    return ((z + 8 + dz) % 8) * 4 + (y + gray(i)) % 4


def forward_group(pairs, block, masks, mask, expanded, keys, square, masking, gamma):
    features = wide_features(block)
    wide = expanded_features(features, mask[...])
    pair_side = jnp.concatenate([expanded[...], expanded_pairs(block, masks)], axis=0)
    both = nt(pairs, pair_side)
    bias, pair_part = both[:, :LANES], both[:, LANES:]
    dots = nt(keys[:, 0:256], wide[:, 0:256])
    cross = nt(keys[:, 256:512], wide[:, 256:512])
    grads = nt(keys[:, 512:1024], wide[:, 512:1024]) + pair_part
    points = features[:, 256:512]
    squares = points * points
    high = squares.astype(BF16).astype(F32)
    pick = mask[:, 256:512]
    parts = jnp.concatenate(
        [expanded_features(high, pick), expanded_features(squares - high, pick)], axis=1
    )
    query_square = nt(jnp.ones((ROWS, 512), BF16), parts)[0:1, :]
    distance = query_square + square[...] - 2.0 * cross
    scores = WL * (dots * 0.25 + bias) - (DIST_WEIGHT * gamma) * distance - masking
    top = jnp.max(scores, axis=0, keepdims=True)
    weights = jnp.exp(scores - top)
    total = jnp.sum(weights, axis=0, keepdims=True)
    inner = jnp.sum(weights * grads, axis=0, keepdims=True)
    return weights, grads, distance, top, total, inner


def combine_stats(arrived, answers, table):
    for d in range(32):
        for n in range(3):
            table[n, d : d + 1, :] = arrived[d, :, n * LANES : (n + 1) * LANES]
    tops = table[0]
    top = jnp.max(tops, axis=0, keepdims=True)
    factors = jnp.exp(tops - top)
    total = jnp.sum(factors * table[1], axis=0, keepdims=True)
    inner = jnp.sum(factors * table[2], axis=0, keepdims=True) / total
    factors = factors / total
    for d in range(32):
        answers[d, :, 0:LANES] = factors[d : d + 1, :]
        answers[d, :, LANES : 2 * LANES] = inner


def score_group(factor, inner, weights, grads, distance):
    probs = weights * factor
    score = probs * (grads - inner)
    head_part = jnp.sum(score * distance, axis=0, keepdims=True)
    return (WL * score).astype(BF16), probs.astype(BF16), head_part


def bias_group(score_half, pairs, flipped):
    turned = score_half.astype(F32).T
    flipped[...] = turned
    bias_part = jnp.zeros((16, LANES), F32)
    for i in range(ROWS):
        rows = flipped[pl.ds(i, 16, stride=ROWS), :].astype(BF16)
        bias_part = bias_part + nn(rows, pairs[i])
    return turned.astype(BF16), bias_part


def small_group(score_half, probs_half, turned, block, mask, head_rows, keys, point_gamma):
    features = wide_features(block)
    wide = expanded_features(features, mask[...])
    key_part = jnp.concatenate(
        [nn(score_half, wide[:, 0:512]), nn(probs_half, wide[:, 512:1024])], axis=1
    )
    key_sum = nn(score_half, mask[:, 256:512])
    product = nn(turned, keys[:, 0:512])
    row_sum = jnp.sum(turned.astype(F32), axis=1, keepdims=True)
    query_part = jnp.zeros((ROWS, 512), F32)
    row_part = jnp.zeros((ROWS, 256), F32)
    for h in range(H):
        at = slice(h * ROWS, (h + 1) * ROWS)
        query_part = query_part + head_rows[at, :] * product[at, :]
        row_part = row_part + head_rows[at, 256:512] * row_sum[at, :]
    vectors = 0.25 * query_part[:, 0:256]
    points = (WC * point_gamma) * (query_part[:, 256:512] - features[:, 256:512] * row_part)
    points = pltpu.roll(points, 64, 1)
    query_out = jnp.concatenate(
        [vectors[:, :128], vectors[:, 128:] + points[:, :128], points[:, 128:]], axis=1
    )
    return key_part, key_sum, query_out


def sum_of(ref, count):
    total = ref[0].astype(F32)
    for k in range(1, count):
        total = total + ref[k].astype(F32)
    return total


def main_kernel(
    loss,
    residues,
    pair_hbm,
    queries,
    qpoints,
    frames,
    keyset,
    kpoints,
    values,
    vpoints,
    key_mask,
    weight,
    head_weight,
    gscalar,
    gpair,
    gpoints,
    halves_out,
    blocks_out,
    query_out,
    key_out,
    total_out,
    pair,
    blocks,
    own_block,
    pieces,
    own_piece,
    piece_rows,
    wide,
    mask,
    head_rows,
    expanded,
    placing,
    keys,
    square,
    weights,
    grads,
    distance,
    stats,
    arrived,
    answers,
    answered,
    table,
    halves,
    turned,
    flipped,
    key_acc,
    sum_acc,
    bias_acc,
    head_acc,
    query_parts,
    query_in,
    key_parts,
    key_in,
    totals,
    row_in,
    y_in,
    z_in,
    pair_sem,
    own_sem,
    out_sem,
    send_sem,
    recv_sem,
    key_send,
    key_recv,
    stats_send,
    stats_recv,
    answer_send,
    answer_recv,
    query_send,
    query_recv,
    part_send,
    part_recv,
    total_send,
    total_recv,
):
    row, col = lax.axis_index("row"), lax.axis_index("col")
    z, y = col // 4, col % 4
    here = (row, col)
    groups = blocks.shape[0]

    def remote(source, target, send, recv, device):
        return pltpu.make_async_remote_copy(source, target, send, recv, device, MESH)

    barrier = pltpu.get_barrier_semaphore()
    for d in range(1, 32):
        pl.semaphore_signal(barrier, 1, device_id=(row, (col + d) % 32), device_id_type=MESH)
    for d in range(1, 8):
        pl.semaphore_signal(barrier, 1, device_id=((row + d) % 8, col), device_id_type=MESH)
    quarter = pair.shape[0] // 4
    pair_copies = []
    for k in range(4):
        at = pl.ds(k * quarter, quarter)
        copy = pltpu.make_async_copy(pair_hbm.at[at], pair.at[at], pair_sem.at[k])
        copy.start()
        pair_copies.append(copy)
    make_block(own_block, queries, qpoints, frames, gscalar, gpair, gpoints, wide, loss)
    make_key_piece(own_piece, keyset, kpoints, values, vpoints, piece_rows)
    pl.semaphore_wait(barrier, 38)

    up = (row, ((z + 1) % 8) * 4 + y)
    down = (row, ((z + 7) % 8) * 4 + y)

    def send_block(source, slot, target, at):
        remote(source, blocks.at[slot], send_sem.at[at], recv_sem.at[slot], target).start()

    def block_arrived(slot):
        remote(own_block, blocks.at[slot], send_sem.at[0], recv_sem.at[slot], here).wait_recv()

    send_block(own_block, col, up, 0)
    send_block(own_block, col, down, 1)
    for n, d in enumerate((1, 3, 2)):
        send_block(own_block, col, (row, z * 4 + (y + d) % 4), 2 + n)
    for d in range(1, 8):
        peer = ((row + d) % 8, col)
        remote(own_piece, pieces.at[row], key_send.at[d], key_recv.at[row], peer).start()
    own_copy = pltpu.make_async_copy(own_block, blocks.at[col], own_sem.at[0])
    own_copy.start()
    piece_copy = pltpu.make_async_copy(own_piece, pieces.at[row], own_sem.at[1])
    piece_copy.start()

    full = head_mask()
    mask[...] = full.astype(BF16)
    head_rows[...] = full[0 : H * ROWS, 0:512]
    fill_weight(expanded, weight[...])
    fill_placing(placing)
    key_acc[...] = jnp.zeros_like(key_acc)
    sum_acc[...] = jnp.zeros_like(sum_acc)
    bias_acc[...] = jnp.zeros_like(bias_acc)
    head_acc[...] = jnp.zeros_like(head_acc)
    masks = residue_masks()
    gamma = softplus_of(per_head(head_weight, lane_heads()))
    point_gamma = softplus_of(per_head(head_weight, feature_heads()[:, 256:512]))
    masking = 100000.0 * (1.0 - key_mask[...].astype(F32))
    masking = jnp.broadcast_to(masking, (ROWS, masking.shape[1])).T[:, 0:1]

    for n, d in enumerate((1, 3, 2)):
        slot = z * 4 + (y + d) % 4
        block_arrived(slot)
        send_block(blocks.at[slot], slot, up, 5 + 2 * n)
        send_block(blocks.at[slot], slot, down, 6 + 2 * n)
    for d in range(1, 8):
        source = (row + d) % 8
        remote(own_piece, pieces.at[source], key_send.at[d], key_recv.at[source], here).wait_recv()
    piece_copy.wait()
    own_copy.wait()
    tall = jnp.concatenate([pieces[r] for r in range(8)], axis=1)
    keys[...] = nn(tall, placing[...]).astype(BF16)
    points = keys[:, 256:512].astype(F32)
    squares = points * points
    high_part = squares.astype(BF16)
    low_part = (squares - high_part.astype(F32)).astype(BF16)
    square[...] = nt(high_part, mask[:, 256:512]) + nt(low_part, mask[:, 256:512])
    for copy in pair_copies:
        copy.wait()

    def send_stats(slot):
        remote(
            stats.at[slot], arrived.at[col], stats_send.at[slot], stats_recv.at[col], (row, slot)
        ).start()

    def forward_one(slot):
        first = pl.multiple_of(slot * ROWS, ROWS)
        pairs = jnp.concatenate([pair[first + i] for i in range(ROWS)], axis=1)
        out = forward_group(
            pairs, blocks[slot], masks, mask, expanded, keys, square, masking, gamma
        )
        weights[slot], grads[slot], distance[slot] = out[0], out[1], out[2]
        for n in range(3):
            stats[slot, :, n * LANES : (n + 1) * LANES] = out[3 + n]

    def forward_step(e, _):
        low, high = ring_slots(e, z, y)

        @pl.when(e >= 2)
        def _():
            block_arrived(low)

        @pl.when((e >= 2) & (e <= 11))
        def _():
            send_block(blocks.at[low], low, up, 11 + e)

        @pl.when(e >= 2)
        def _():
            block_arrived(high)

        @pl.when(((e >= 2) & (e <= 9)) | ((e >= 12) & (e <= 13)))
        def _():
            send_block(blocks.at[high], high, down, 23 + e)

        @pl.when(e >= 1)
        def _():
            send_stats(ring_slots(e - 1, z, y)[0])

        @pl.when(e >= 2)
        def _():
            send_stats(ring_slots(e - 1, z, y)[1])

        forward_one(low)
        forward_one(high)
        return 0

    lax.fori_loop(0, 16, forward_step, 0)
    blocks_copy = pltpu.make_async_copy(blocks, blocks_out, out_sem.at[0])
    blocks_copy.start()
    arrived[col] = stats[col]
    for slot in ring_slots(15, z, y):
        send_stats(slot)

    def stats_arrived(d, _):
        peer = (col + d) % 32
        remote(
            stats.at[peer], arrived.at[peer], stats_send.at[peer], stats_recv.at[peer], here
        ).wait_recv()
        return 0

    lax.fori_loop(1, 32, stats_arrived, 0)
    combine_stats(arrived, answers, table)

    def send_answer(n, _):
        peer = near_slot(32 - n, z, y)
        remote(
            answers.at[peer], answered.at[col], answer_send.at[peer], answer_recv.at[col], (row, peer)
        ).start()
        return 0

    lax.fori_loop(1, 32, send_answer, 0)
    answered[col] = answers[col]

    def score_one(slot, k):
        first = pl.multiple_of(slot * ROWS, ROWS)
        pairs = [pair[first + i] for i in range(ROWS)]
        score_half, probs_half, head_part = score_group(
            answered[slot, :, 0:LANES],
            answered[slot, :, LANES : 2 * LANES],
            weights[slot],
            grads[slot],
            distance[slot],
        )
        halves[slot, :, 0:LANES] = score_half
        halves[slot, :, LANES : 2 * LANES] = probs_half
        turned[slot], bias_part = bias_group(score_half, pairs, flipped.at[k])
        return bias_part, head_part

    def answer_arrived(slot):
        remote(
            answers.at[slot], answered.at[slot], answer_send.at[slot], answer_recv.at[slot], here
        ).wait_recv()

    def score_step(e, _):
        first, second = near_slot(2 * e, z, y), near_slot(2 * e + 1, z, y)

        @pl.when(e >= 1)
        def _():
            answer_arrived(first)

        answer_arrived(second)
        bias_a, head_a = score_one(first, 0)
        bias_b, head_b = score_one(second, 1)
        bias_acc[...] += bias_a + bias_b
        head_acc[...] += head_a + head_b
        return 0

    lax.fori_loop(0, 16, score_step, 0)
    halves_copy = pltpu.make_async_copy(halves, halves_out, out_sem.at[1])
    halves_copy.start()
    totals[0, 0:16, :] = bias_acc[...]
    totals[0, 16:24, :] = jnp.broadcast_to(head_acc[...], (ROWS, LANES))

    def spread_total(source, target, me, count, base, device):
        for d in range(1, count):
            remote(
                source,
                target.at[me],
                total_send.at[base + d],
                total_recv.at[base + me],
                device((me + d) % count),
            ).start()

    def total_arrived(source, target, me, count, base):
        for d in range(1, count):
            peer = (me + d) % count
            remote(
                source, target.at[peer], total_send.at[base + d], total_recv.at[base + peer], here
            ).wait_recv()

    spread_total(totals.at[0], row_in, row, 8, 0, lambda p: (p, col))
    row_in[row] = totals[0]

    def send_query(slot):
        remote(
            query_parts.at[slot], query_in.at[col], query_send.at[slot], query_recv.at[col], (row, slot)
        ).start()

    def small_one(slot):
        out = small_group(
            halves[slot, :, 0:LANES],
            halves[slot, :, LANES : 2 * LANES],
            turned[slot],
            blocks[slot],
            mask,
            head_rows,
            keys,
            point_gamma,
        )
        query_parts[slot] = out[2].astype(BF16)
        return out[0], out[1]

    def small_step(e, _):
        first, second = near_slot(31 - 2 * e, z, y), near_slot(30 - 2 * e, z, y)

        @pl.when(e >= 1)
        def _():
            send_query(near_slot(33 - 2 * e, z, y))
            send_query(near_slot(32 - 2 * e, z, y))

        key_a, sum_a = small_one(first)
        key_b, sum_b = small_one(second)
        key_acc[...] += key_a + key_b
        sum_acc[...] += sum_a + sum_b
        return 0

    lax.fori_loop(0, 8, small_step, 0)
    total_arrived(totals.at[0], row_in, row, 8, 0)
    totals[1] = sum_of(row_in, 8)
    y_in[y] = totals[1]
    spread_total(totals.at[1], y_in, y, 4, 8, lambda p: (row, z * 4 + p))
    lax.fori_loop(8, 16, small_step, 0)
    send_query(near_slot(1, z, y))
    query_in[col] = query_parts[col]
    total_arrived(totals.at[1], y_in, y, 4, 8)
    totals[2] = sum_of(y_in, 4)
    z_in[z] = totals[2]
    spread_total(totals.at[2], z_in, z, 8, 12, lambda p: (row, p * 4 + y))
    key_points = (WC * point_gamma) * (
        key_acc[:, 256:512] - keys[:, 256:512].astype(F32) * sum_acc[...]
    )
    whole = jnp.concatenate(
        [0.25 * key_acc[:, 0:256], key_points, key_acc[:, 512:1024]], axis=1
    ).astype(BF16)
    spread = nt(whole, placing[...])
    for r in range(8):
        key_parts[r] = spread[:, r * LANES : (r + 1) * LANES].astype(BF16)
    key_in[row] = key_parts[row]
    for d in range(1, 8):
        peer = (row + d) % 8
        remote(
            key_parts.at[peer], key_in.at[row], part_send.at[d], part_recv.at[row], (peer, col)
        ).start()

    def query_arrived(d, _):
        peer = (col + d) % 32
        remote(
            query_parts.at[peer], query_in.at[peer], query_send.at[peer], query_recv.at[peer], here
        ).wait_recv()
        return 0

    lax.fori_loop(1, 32, query_arrived, 0)
    mine = sum_of(query_in, 32)
    query_out[:, 0:256] = mine[:, 0:256]
    back = pltpu.roll(mine, 384 - 192, 1)[:, 0:256]
    lane = iota((ROWS, 256), 1)
    back = jnp.where(lane < 3.0 * H * PQ, back, 0.0)
    query_out[:, 256:512] = rotated(frames[...], back, 256, True)
    for d in range(1, 8):
        peer = (row + d) % 8
        remote(
            key_parts.at[peer], key_in.at[peer], part_send.at[d], part_recv.at[peer], here
        ).wait_recv()
    key_out[...] = sum_of(key_in, 8).T
    total_arrived(totals.at[2], z_in, z, 8, 12)
    total_out[...] = sum_of(z_in, 8)

    for at in list(range(11)) + list(range(13, 23)) + list(range(25, 33)) + [35, 36]:
        remote(own_block, blocks.at[0], send_sem.at[at], recv_sem.at[0], here).wait_send()
    for d in range(1, 8):
        remote(own_piece, pieces.at[0], key_send.at[d], key_recv.at[0], here).wait_send()
        remote(key_parts.at[0], key_in.at[0], part_send.at[d], part_recv.at[0], here).wait_send()

    def all_left(d, _):
        peer = (col + d) % 32
        remote(
            stats.at[peer], arrived.at[peer], stats_send.at[peer], stats_recv.at[peer], here
        ).wait_send()
        remote(
            answers.at[peer], answered.at[peer], answer_send.at[peer], answer_recv.at[peer], here
        ).wait_send()
        remote(
            query_parts.at[peer], query_in.at[peer], query_send.at[peer], query_recv.at[peer], here
        ).wait_send()
        return 0

    lax.fori_loop(1, 32, all_left, 0)
    for base, count in ((0, 8), (8, 4), (12, 8)):
        for d in range(1, count):
            remote(
                totals.at[0], row_in.at[0], total_send.at[base + d], total_recv.at[0], here
            ).wait_send()
    blocks_copy.wait()
    halves_copy.wait()


def last_kernel(
    steps,
    residues,
    halves,
    blocks,
    weight,
    head_weight,
    query_sum,
    key_sum,
    total_sum,
    pair_grad,
    queries_grad,
    qpoints_grad,
    keyset_grad,
    kpoints_grad,
    values_grad,
    vpoints_grad,
    bias_grad,
    head_grad,
    expanded,
):
    @pl.when(pl.program_id(0) == 0)
    def _():
        fill_weight(expanded, weight[...])
        queries_grad[...] = query_sum[:, 0:192]
        qpoints_grad[...] = query_sum[:, 256:400]
        at = 0
        for out in (keyset_grad, kpoints_grad, values_grad, vpoints_grad):
            out[...] = key_sum[at : at + out.shape[0], :]
            at += out.shape[0]
        bias_grad[...] = total_sum[0:H, :] * (1.0 / residues)
        heads = lane_heads()
        raw = per_head(head_weight, heads)
        line = total_sum[16:17, :] * (-DIST_WEIGHT / residues) / (1.0 + jnp.exp(-raw))
        for h in range(H):
            head_grad[h] = jnp.sum(jnp.where(heads == float(h), line, 0.0))

    masks = residue_masks()
    for k in range(steps):
        pair_side = jnp.concatenate([expanded[...], expanded_pairs(blocks[k], masks)], axis=0)
        out = nn(halves[k], pair_side)
        for i in range(ROWS):
            pair_grad[k * ROWS + i] = out[:, i * LANES : (i + 1) * LANES].astype(BF16)


def shape(*dims, dtype=F32):
    return jax.ShapeDtypeStruct(dims, dtype)


VMEM = pl.BlockSpec(memory_space=pltpu.VMEM)
SMEM = pl.BlockSpec(memory_space=pltpu.SMEM)
ANY = pl.BlockSpec(memory_space=pl.ANY)
DMA = pltpu.SemaphoreType.DMA
STEPS = 4


def local(
    pair_rep,
    queries,
    qpoints,
    frames,
    keyset,
    kpoints,
    values,
    vpoints,
    key_mask,
    bias_weight,
    head_weight,
    grad_scalar,
    grad_pair,
    grad_points,
):
    rows, keys, _ = pair_rep.shape
    residues = queries.shape[0] * 256
    loss = float(residues // 16)
    groups = rows // ROWS
    weight = bias_weight.T
    full, half = pltpu.VMEM, lambda *dims: pltpu.VMEM(dims, BF16)
    halves, blocks, query_sum, key_sum, total_sum = pl.pallas_call(
        functools.partial(main_kernel, loss, float(residues)),
        out_shape=(
            shape(groups, keys, 2 * LANES, dtype=BF16),
            shape(groups, 160, LANES, dtype=BF16),
            shape(ROWS, 512),
            shape(LANES, keys),
            shape(24, LANES),
        ),
        in_specs=[ANY] + [VMEM] * 9 + [SMEM] + [VMEM] * 3,
        out_specs=(ANY, ANY, VMEM, VMEM, VMEM),
        scratch_shapes=[
            half(rows, keys, LANES),
            half(groups, 160, LANES),
            half(160, LANES),
            half(8, keys, LANES),
            half(keys, LANES),
            full((LANES, keys), F32),
            full((ROWS, 384), F32),
            half(LANES, FEATURES),
            full((H * ROWS, 512), F32),
            half(LANES, FEATURES),
            half(FEATURES, FEATURES),
            half(keys, FEATURES),
            full((keys, LANES), F32),
            full((groups, keys, LANES), F32),
            full((groups, keys, LANES), F32),
            full((groups, keys, LANES), F32),
            full((groups, 1, 3 * LANES), F32),
            full((groups, 1, 3 * LANES), F32),
            full((groups, 1, 2 * LANES), F32),
            full((groups, 1, 2 * LANES), F32),
            full((3, groups, LANES), F32),
            half(groups, keys, 2 * LANES),
            half(groups, LANES, keys),
            full((2, LANES, keys), F32),
            full((keys, FEATURES), F32),
            full((keys, 256), F32),
            full((16, LANES), F32),
            full((1, LANES), F32),
            half(groups, ROWS, 384),
            half(groups, ROWS, 384),
            half(8, keys, LANES),
            half(8, keys, LANES),
            full((3, 24, LANES), F32),
            full((8, 24, LANES), F32),
            full((4, 24, LANES), F32),
            full((8, 24, LANES), F32),
            DMA((4,)),
            DMA((2,)),
            DMA((2,)),
            DMA((40,)),
            DMA((32,)),
            DMA((8,)),
            DMA((8,)),
            DMA((32,)),
            DMA((32,)),
            DMA((32,)),
            DMA((32,)),
            DMA((32,)),
            DMA((32,)),
            DMA((8,)),
            DMA((8,)),
            DMA((20,)),
            DMA((20,)),
        ],
        compiler_params=pltpu.CompilerParams(
            collective_id=0, has_side_effects=True, vmem_limit_bytes=40 << 20
        ),
        name="main",
    )(
        pair_rep,
        queries,
        qpoints,
        frames,
        keyset.T,
        kpoints.T,
        values.T,
        vpoints.T,
        key_mask.reshape(1, keys),
        weight,
        head_weight,
        grad_scalar,
        grad_pair,
        grad_points,
    )
    per_step = lambda *dims: pl.BlockSpec((STEPS, *dims), lambda g: (g,) + (0,) * len(dims))
    whole = lambda *dims: pl.BlockSpec(dims, lambda g: (0,) * len(dims))
    finals = (
        (ROWS, H * C),
        (ROWS, 3 * H * PQ),
        (24, keys),
        (18, keys),
        (24, keys),
        (36, keys),
        (H, CZ),
    )
    pair_grad, queries_grad, qpoints_grad, *turned, bias_grad, head_grad = pl.pallas_call(
        functools.partial(last_kernel, STEPS, float(residues)),
        grid=(groups // STEPS,),
        out_shape=(
            shape(rows, keys, LANES, dtype=BF16),
            *(shape(*dims) for dims in finals),
            shape(H),
        ),
        in_specs=[
            per_step(keys, 2 * LANES),
            per_step(160, LANES),
            whole(H, CZ),
            SMEM,
            whole(ROWS, 512),
            whole(LANES, keys),
            whole(24, LANES),
        ],
        out_specs=(
            pl.BlockSpec((STEPS * ROWS, keys, LANES), lambda g: (g, 0, 0)),
            *(whole(*dims) for dims in finals),
            SMEM,
        ),
        scratch_shapes=[half(LANES, FEATURES)],
        name="last",
    )(halves, blocks, weight, head_weight, query_sum, key_sum, total_sum)
    return (
        pair_grad,
        queries_grad,
        qpoints_grad,
        *(array.T for array in turned),
        bias_grad.T,
        head_grad,
    )


def solution(mesh):
    both = ("row", "col")
    return jax.shard_map(
        local,
        mesh=mesh,
        in_specs=(
            P("row", "col", None),
            P(both, None),
            P(both, None),
            P(both, None),
            P("col", "row"),
            P("col", "row"),
            P("col", "row"),
            P("col", "row"),
            P("col"),
            P(),
            P(),
            P(both, None),
            P(both, None),
            P(both, None),
        ),
        out_specs=(
            P("row", "col", None),
            P(both, None),
            P(both, None),
            P("col", "row"),
            P("col", "row"),
            P("col", "row"),
            P("col", "row"),
            P(),
            P(),
        ),
        check_vma=False,
    )
```

profile of v0, /device:TPU:1, one launch (start us, length us, event | category | flops | bytes accessed | tf_op | source)
XLA Modules:
  0.0 88.7 jit_solution(10166241437638521057)
XLA Ops:
  0.6 0.0 copy-start
  0.7 2.2 %copy-done = bf16[256,64,128]{2,1,0:T(8,128)(2,1)S(1)} copy-done((bf16[256,64,128]{2,1,0:T(8,128)(2,1)S(1)}, bf16[256,64,128]{2,1,0:T(8,128)(2,1)}, u32[]{:S(2)}) %copy-start) | copy-done | bytes 4194328
  2.8 0.0 copy-start.4
  2.8 0.7 copy-done.4
  3.6 0.7 copy-done.6
  4.3 0.7 copy-done.8
  5.0 0.7 copy-done.9
  5.7 0.7 copy-done.10
  6.3 0.7 copy-done.11
  7.0 0.7 copy-done.12
  7.7 0.7 copy-done.13
  8.4 0.7 copy-done.14
  9.1 0.7 copy-done.15
  9.8 0.7 copy-done.16
  10.5 0.7 copy-done.17
  11.1 0.7 copy-done.18
  11.8 64.9 %main.1 = (bf16[32,64,256]{2,1,0:T(8,128)(2,1)S(1)}, bf16[32,160,128]{2,1,0:T(8,128)(2,1)S(1)}, f32[8,512]{1,0:T(8,128)S(1)}, f32[128,64]{1,0:T(8,128)S(1)}, f32[24,128]{1,0:T(8,128)S(1)}) custom-call(bf16[256,64,128]{2,1,0:T(8,128)(2,1)S(1)} %copy-done, bf16[8,192]{1,0:T(8,128)(2,1)S(1)} %copy-done.13, bf16[8,144]{1,0:T(8,128)(2,1)S(1)} %copy-done.14, ...), custom_call_target="tpu_custom_call" | custom-call | tf_op jit(solution)/shard_map/main/pallas_call | solution.py:764
  76.7 0.0 copy-start.1
  76.7 1.1 %copy-done.1 = bf16[32,160,128]{2,1,0:T(8,128)(2,1)} copy-done((bf16[32,160,128]{2,1,0:T(8,128)(2,1)}, bf16[32,160,128]{2,1,0:T(8,128)(2,1)S(1)}, u32[]{:S(2)}) %copy-start.1) | copy-done | bytes 1310744
  77.8 1.0 %copy-done.2 = bf16[32,64,256]{2,1,0:T(8,128)(2,1)} copy-done((bf16[32,64,256]{2,1,0:T(8,128)(2,1)}, bf16[32,64,256]{2,1,0:T(8,128)(2,1)S(1)}, u32[]{:S(2)}) %copy-start.2) | copy-done | bytes 1048600
  78.7 0.6 copy-done.3
  79.3 0.6 copy-done.5
  79.9 0.6 copy-done.7
  80.5 8.2 %last.1 = (bf16[256,64,128]{2,1,0:T(8,128)(2,1)}, f32[8,192]{1,0:T(8,128)}, f32[8,144]{1,0:T(8,128)}, f32[24,64]{1,0:T(8,128)}, f32[18,64]{1,0:T(8,128)}, /*inde...) custom-call(bf16[32,64,256]{2,1,0:T(8,128)(2,1)} %copy-done.2, ...), custom_call_target="tpu_custom_call" | custom-call | tf_op jit(solution)/shard_map/last/pallas_call | solution.py:861
  (16 shorter events, 0.0 us)
Async XLA Ops:
  0.6 2.2 %copy-start = (bf16[256,64,128]{2,1,0:T(8,128)(2,1)S(1)}, bf16[256,64,128]{2,1,0:T(8,128)(2,1)}, u32[]{:S(2)}) copy-start(bf16[256,64,128]{2,1,0:T(8,128)(2,1)} %pair_hbm.1) | copy-start | bytes 12582916
  2.8 0.7 copy-start.4
  3.6 0.7 copy-start.6
  4.3 0.7 copy-start.8
  5.0 0.7 copy-start.9
  5.7 0.7 copy-start.10
  6.3 0.7 copy-start.11
  7.0 0.7 copy-start.12
  7.7 0.7 copy-start.13
  8.4 0.7 copy-start.14
  9.1 0.7 copy-start.15
  9.8 0.7 copy-start.16
  10.5 0.7 copy-start.17
  11.1 0.7 copy-start.18
  76.7 1.1 %copy-start.1 = (bf16[32,160,128]{2,1,0:T(8,128)(2,1)}, bf16[32,160,128]{2,1,0:T(8,128)(2,1)S(1)}, u32[]{:S(2)}) copy-start(bf16[32,160,128]{2,1,0:T(8,128)(2,1)S(1)} %get-tuple-element.24.blocks) | copy-start | bytes 3932164
  77.8 1.0 %copy-start.2 = (bf16[32,64,256]{2,1,0:T(8,128)(2,1)}, bf16[32,64,256]{2,1,0:T(8,128)(2,1)S(1)}, u32[]{:S(2)}) copy-start(bf16[32,64,256]{2,1,0:T(8,128)(2,1)S(1)} %get-tuple-element.23.halves) | copy-start | bytes 3145732
  78.7 0.6 copy-start.3
  79.3 0.6 copy-start.5
  79.9 0.6 copy-start.7
where the time goes:
time: 89.4 us; the launch traced here: 88.7 us
  Pallas kernels  73.1 us (82%)
  local copies, waits for them, and re-layouts  15 us (17%)
    pallas_call x1, Pallas kernels, local(): pl.pallas_call(functools.partial(main_kernel, loss, float(residues)), out...  64.9 us
    unnamed x38, local copies, waits for them, and re-layouts  15 us
    pallas_call x1, Pallas kernels, local(): pl.pallas_call(functools.partial(last_kernel, STEPS, float(residues)), gr...  8.18 us

commit v1 on v0

--- a/solution.py
+++ b/solution.py
@@ -104,7 +104,7 @@
 def per_head(values, heads):
     total = jnp.zeros(heads.shape, F32)
     for h in range(H):
-        total = jnp.where(heads == float(h), values[h], total)
+        total = jnp.where(heads == float(h), values[:, h : h + 1], total)
     return total
 
 
@@ -285,6 +285,23 @@
     loss,
     residues,
     pair_hbm,
+    queries_hbm,
+    qpoints_hbm,
+    frames_hbm,
+    keyset_hbm,
+    kpoints_hbm,
+    values_hbm,
+    vpoints_hbm,
+    key_mask_hbm,
+    weight_hbm,
+    head_weight_hbm,
+    gscalar_hbm,
+    gpair_hbm,
+    gpoints_hbm,
+    pair_out,
+    query_out,
+    key_out,
+    total_out,
     queries,
     qpoints,
     frames,
@@ -298,11 +315,6 @@
     gscalar,
     gpair,
     gpoints,
-    halves_out,
-    blocks_out,
-    query_out,
-    key_out,
-    total_out,
     pair,
     blocks,
     own_block,
@@ -325,6 +337,7 @@
     answered,
     table,
     halves,
+    pair_stage,
     turned,
     flipped,
     key_acc,
@@ -339,6 +352,7 @@
     row_in,
     y_in,
     z_in,
+    input_sem,
     pair_sem,
     own_sem,
     out_sem,
@@ -366,10 +380,34 @@
         return pltpu.make_async_remote_copy(source, target, send, recv, device, MESH)
 
     barrier = pltpu.get_barrier_semaphore()
-    for d in range(1, 32):
-        pl.semaphore_signal(barrier, 1, device_id=(row, (col + d) % 32), device_id_type=MESH)
+    for d in (1, 2, 3):
+        pl.semaphore_signal(barrier, 1, device_id=(row, z * 4 + (y + d) % 4), device_id_type=MESH)
+    for d in (1, 7):
+        pl.semaphore_signal(
+            barrier, 1, device_id=(row, ((z + d) % 8) * 4 + y), device_id_type=MESH
+        )
     for d in range(1, 8):
         pl.semaphore_signal(barrier, 1, device_id=((row + d) % 8, col), device_id_type=MESH)
+    inputs = (
+        (queries_hbm, queries),
+        (qpoints_hbm, qpoints),
+        (frames_hbm, frames),
+        (keyset_hbm, keyset),
+        (kpoints_hbm, kpoints),
+        (values_hbm, values),
+        (vpoints_hbm, vpoints),
+        (key_mask_hbm, key_mask),
+        (weight_hbm, weight),
+        (head_weight_hbm, head_weight),
+        (gscalar_hbm, gscalar),
+        (gpair_hbm, gpair),
+        (gpoints_hbm, gpoints),
+    )
+    input_copies = []
+    for k, (source, target) in enumerate(inputs):
+        copy = pltpu.make_async_copy(source, target, input_sem.at[k])
+        copy.start()
+        input_copies.append(copy)
     quarter = pair.shape[0] // 4
     pair_copies = []
     for k in range(4):
@@ -377,9 +415,11 @@
         copy = pltpu.make_async_copy(pair_hbm.at[at], pair.at[at], pair_sem.at[k])
         copy.start()
         pair_copies.append(copy)
+    for copy in input_copies:
+        copy.wait()
     make_block(own_block, queries, qpoints, frames, gscalar, gpair, gpoints, wide, loss)
     make_key_piece(own_piece, keyset, kpoints, values, vpoints, piece_rows)
-    pl.semaphore_wait(barrier, 38)
+    pl.semaphore_wait(barrier, 12)
 
     up = (row, ((z + 1) % 8) * 4 + y)
     down = (row, ((z + 7) % 8) * 4 + y)
@@ -484,8 +524,6 @@
         return 0
 
     lax.fori_loop(0, 16, forward_step, 0)
-    blocks_copy = pltpu.make_async_copy(blocks, blocks_out, out_sem.at[0])
-    blocks_copy.start()
     arrived[col] = stats[col]
     for slot in ring_slots(15, z, y):
         send_stats(slot)
@@ -500,14 +538,16 @@
     lax.fori_loop(1, 32, stats_arrived, 0)
     combine_stats(arrived, answers, table)
 
-    def send_answer(n, _):
-        peer = near_slot(32 - n, z, y)
-        remote(
-            answers.at[peer], answered.at[col], answer_send.at[peer], answer_recv.at[col], (row, peer)
-        ).start()
-        return 0
-
-    lax.fori_loop(1, 32, send_answer, 0)
+    for d in range(16, 48):
+        if d != 32:
+            peer = (col + d) % 32
+            remote(
+                answers.at[peer],
+                answered.at[col],
+                answer_send.at[peer],
+                answer_recv.at[col],
+                (row, peer),
+            ).start()
     answered[col] = answers[col]
 
     def score_one(slot, k):
@@ -545,8 +585,6 @@
         return 0
 
     lax.fori_loop(0, 16, score_step, 0)
-    halves_copy = pltpu.make_async_copy(halves, halves_out, out_sem.at[1])
-    halves_copy.start()
     totals[0, 0:16, :] = bias_acc[...]
     totals[0, 16:24, :] = jnp.broadcast_to(head_acc[...], (ROWS, LANES))
 
@@ -603,7 +641,27 @@
         sum_acc[...] += sum_a + sum_b
         return 0
 
+    def stage_copy(slot):
+        at = pl.ds(pl.multiple_of(slot * ROWS, ROWS), ROWS)
+        return pltpu.make_async_copy(pair_stage.at[at], pair_out.at[at], out_sem.at[slot])
+
+    def pair_step(e, _):
+        @pl.when(e >= 1)
+        def _():
+            stage_copy(2 * e - 2).start()
+            stage_copy(2 * e - 1).start()
+
+        for k in range(2):
+            slot = 2 * e + k
+            first = pl.multiple_of(slot * ROWS, ROWS)
+            side = jnp.concatenate([expanded[...], expanded_pairs(blocks[slot], masks)], axis=0)
+            out = nn(halves[slot], side)
+            for i in range(ROWS):
+                pair_stage[first + i] = out[:, i * LANES : (i + 1) * LANES].astype(BF16)
+        return 0
+
     lax.fori_loop(0, 8, small_step, 0)
+    lax.fori_loop(0, 2, pair_step, 0)
     total_arrived(totals.at[0], row_in, row, 8, 0)
     totals[1] = sum_of(row_in, 8)
     y_in[y] = totals[1]
@@ -631,6 +689,8 @@
             key_parts.at[peer], key_in.at[row], part_send.at[d], part_recv.at[row], (peer, col)
         ).start()
 
+    lax.fori_loop(2, 16, pair_step, 0)
+
     def query_arrived(d, _):
         peer = (col + d) % 32
         remote(
@@ -651,6 +711,8 @@
             key_parts.at[peer], key_in.at[peer], part_send.at[d], part_recv.at[peer], here
         ).wait_recv()
     key_out[...] = sum_of(key_in, 8).T
+    stage_copy(groups - 2).start()
+    stage_copy(groups - 1).start()
     total_arrived(totals.at[2], z_in, z, 8, 12)
     total_out[...] = sum_of(z_in, 8)
 
@@ -679,16 +741,17 @@
             remote(
                 totals.at[0], row_in.at[0], total_send.at[base + d], total_recv.at[0], here
             ).wait_send()
-    blocks_copy.wait()
-    halves_copy.wait()
+
+    def stage_left(slot, _):
+        stage_copy(slot).wait()
+        return 0
+
+    lax.fori_loop(0, groups, stage_left, 0)
 
 
 def last_kernel(
-    steps,
     residues,
-    halves,
-    blocks,
-    weight,
+    pair_in,
     head_weight,
     query_sum,
     key_sum,
@@ -702,30 +765,35 @@
     vpoints_grad,
     bias_grad,
     head_grad,
-    expanded,
+    stage,
+    in_sem,
+    out_sem,
 ):
-    @pl.when(pl.program_id(0) == 0)
-    def _():
-        fill_weight(expanded, weight[...])
-        queries_grad[...] = query_sum[:, 0:192]
-        qpoints_grad[...] = query_sum[:, 256:400]
-        at = 0
-        for out in (keyset_grad, kpoints_grad, values_grad, vpoints_grad):
-            out[...] = key_sum[at : at + out.shape[0], :]
-            at += out.shape[0]
-        bias_grad[...] = total_sum[0:H, :] * (1.0 / residues)
-        heads = lane_heads()
-        raw = per_head(head_weight, heads)
-        line = total_sum[16:17, :] * (-DIST_WEIGHT / residues) / (1.0 + jnp.exp(-raw))
-        for h in range(H):
-            head_grad[h] = jnp.sum(jnp.where(heads == float(h), line, 0.0))
-
-    masks = residue_masks()
-    for k in range(steps):
-        pair_side = jnp.concatenate([expanded[...], expanded_pairs(blocks[k], masks)], axis=0)
-        out = nn(halves[k], pair_side)
-        for i in range(ROWS):
-            pair_grad[k * ROWS + i] = out[:, i * LANES : (i + 1) * LANES].astype(BF16)
+    pieces = in_sem.shape[0]
+    size = stage.shape[0] // pieces
+    arrivals, leaves = [], []
+    for k in range(pieces):
+        at = pl.ds(k * size, size)
+        arrivals.append(pltpu.make_async_copy(pair_in.at[at], stage.at[at], in_sem.at[k]))
+        leaves.append(pltpu.make_async_copy(stage.at[at], pair_grad.at[at], out_sem.at[k]))
+        arrivals[k].start()
+    queries_grad[...] = query_sum[:, 0:192]
+    qpoints_grad[...] = query_sum[:, 256:400]
+    at = 0
+    for out in (keyset_grad, kpoints_grad, values_grad, vpoints_grad):
+        out[...] = key_sum[at : at + out.shape[0], :]
+        at += out.shape[0]
+    bias_grad[...] = total_sum[0:H, :] * (1.0 / residues)
+    heads = lane_heads()
+    raw = per_head(head_weight, heads)
+    line = total_sum[16:17, :] * (-DIST_WEIGHT / residues) / (1.0 + jnp.exp(-raw))
+    for h in range(H):
+        head_grad[h] = jnp.sum(jnp.where(heads == float(h), line, 0.0))
+    for k in range(pieces):
+        arrivals[k].wait()
+        leaves[k].start()
+    for k in range(pieces):
+        leaves[k].wait()
 
 
 def shape(*dims, dtype=F32):
@@ -735,8 +803,8 @@
 VMEM = pl.BlockSpec(memory_space=pltpu.VMEM)
 SMEM = pl.BlockSpec(memory_space=pltpu.SMEM)
 ANY = pl.BlockSpec(memory_space=pl.ANY)
+HBM = pl.BlockSpec(memory_space=pltpu.HBM)
 DMA = pltpu.SemaphoreType.DMA
-STEPS = 4
 
 
 def local(
@@ -761,18 +829,33 @@
     groups = rows // ROWS
     weight = bias_weight.T
     full, half = pltpu.VMEM, lambda *dims: pltpu.VMEM(dims, BF16)
-    halves, blocks, query_sum, key_sum, total_sum = pl.pallas_call(
+    given = (
+        queries,
+        qpoints,
+        frames,
+        keyset.T,
+        kpoints.T,
+        values.T,
+        vpoints.T,
+        key_mask.reshape(1, keys),
+        weight,
+        head_weight.reshape(1, H),
+        grad_scalar,
+        grad_pair,
+        grad_points,
+    )
+    pair_main, query_sum, key_sum, total_sum = pl.pallas_call(
         functools.partial(main_kernel, loss, float(residues)),
         out_shape=(
-            shape(groups, keys, 2 * LANES, dtype=BF16),
-            shape(groups, 160, LANES, dtype=BF16),
+            shape(rows, keys, LANES, dtype=BF16),
             shape(ROWS, 512),
             shape(LANES, keys),
             shape(24, LANES),
         ),
-        in_specs=[ANY] + [VMEM] * 9 + [SMEM] + [VMEM] * 3,
-        out_specs=(ANY, ANY, VMEM, VMEM, VMEM),
+        in_specs=[HBM] * (1 + len(given)),
+        out_specs=(HBM, VMEM, VMEM, VMEM),
         scratch_shapes=[
+            *(full(array.shape, array.dtype) for array in given),
             half(rows, keys, LANES),
             half(groups, 160, LANES),
             half(160, LANES),
@@ -795,6 +878,7 @@
             full((groups, 1, 2 * LANES), F32),
             full((3, groups, LANES), F32),
             half(groups, keys, 2 * LANES),
+            half(rows, keys, LANES),
             half(groups, LANES, keys),
             full((2, LANES, keys), F32),
             full((keys, FEATURES), F32),
@@ -809,9 +893,10 @@
             full((8, 24, LANES), F32),
             full((4, 24, LANES), F32),
             full((8, 24, LANES), F32),
+            DMA((len(given),)),
             DMA((4,)),
             DMA((2,)),
-            DMA((2,)),
+            DMA((groups,)),
             DMA((40,)),
             DMA((32,)),
             DMA((8,)),
@@ -828,27 +913,10 @@
             DMA((20,)),
         ],
         compiler_params=pltpu.CompilerParams(
-            collective_id=0, has_side_effects=True, vmem_limit_bytes=40 << 20
+            collective_id=0, has_side_effects=True, vmem_limit_bytes=67043328
         ),
         name="main",
-    )(
-        pair_rep,
-        queries,
-        qpoints,
-        frames,
-        keyset.T,
-        kpoints.T,
-        values.T,
-        vpoints.T,
-        key_mask.reshape(1, keys),
-        weight,
-        head_weight,
-        grad_scalar,
-        grad_pair,
-        grad_points,
-    )
-    per_step = lambda *dims: pl.BlockSpec((STEPS, *dims), lambda g: (g,) + (0,) * len(dims))
-    whole = lambda *dims: pl.BlockSpec(dims, lambda g: (0,) * len(dims))
+    )(pair_rep, *given)
     finals = (
         (ROWS, H * C),
         (ROWS, 3 * H * PQ),
@@ -859,30 +927,18 @@
         (H, CZ),
     )
     pair_grad, queries_grad, qpoints_grad, *turned, bias_grad, head_grad = pl.pallas_call(
-        functools.partial(last_kernel, STEPS, float(residues)),
-        grid=(groups // STEPS,),
+        functools.partial(last_kernel, float(residues)),
         out_shape=(
             shape(rows, keys, LANES, dtype=BF16),
             *(shape(*dims) for dims in finals),
             shape(H),
         ),
-        in_specs=[
-            per_step(keys, 2 * LANES),
-            per_step(160, LANES),
-            whole(H, CZ),
-            SMEM,
-            whole(ROWS, 512),
-            whole(LANES, keys),
-            whole(24, LANES),
-        ],
-        out_specs=(
-            pl.BlockSpec((STEPS * ROWS, keys, LANES), lambda g: (g, 0, 0)),
-            *(whole(*dims) for dims in finals),
-            SMEM,
-        ),
-        scratch_shapes=[half(LANES, FEATURES)],
+        in_specs=[HBM] + [VMEM] * 4,
+        out_specs=(HBM,) + (VMEM,) * 7 + (SMEM,),
+        scratch_shapes=[half(rows, keys, LANES), DMA((8,)), DMA((8,))],
+        compiler_params=pltpu.CompilerParams(vmem_limit_bytes=67043328),
         name="last",
-    )(halves, blocks, weight, head_weight, query_sum, key_sum, total_sum)
+    )(pair_main, head_weight.reshape(1, H), query_sum, key_sum, total_sum)
     return (
         pair_grad,
         queries_grad,

time: 89.4 us -> 69.6 us (0.78)
  local copies, waits for them, and re-layouts: 15 us -> 0 us
  Pallas kernels: 73.1 us -> 68.7 us
    unnamed x38 -> x0, local copies, waits for them, and re-layouts: 15 us -> none
    pallas_call x1, Pallas kernels: 8.18 us -> 5.1 us  [local(): pl.pallas_call(functools.partial(last_kernel, float(residues)), out_shape...]
    pallas_call x1, Pallas kernels: 64.9 us -> 63.6 us  [local(): pl.pallas_call(functools.partial(main_kernel, loss, float(residues)), out...]
where the time goes in v1:
time: 69.6 us; the launch traced here: 69.4 us
  Pallas kernels  68.7 us (99%)
    pallas_call x1, Pallas kernels, local(): pl.pallas_call(functools.partial(main_kernel, loss, float(residues)), out...  63.6 us
    pallas_call x1, Pallas kernels, local(): pl.pallas_call(functools.partial(last_kernel, float(residues)), out_shape...  5.1 us

profile of v1, /device:TPU:1, one launch (start us, length us, event | category | flops | bytes accessed | tf_op | source)
XLA Modules:
  0.0 69.4 jit_solution(770704354467911071)
XLA Ops:
  0.6 63.6 %main.1 = (bf16[256,64,128]{2,1,0:T(8,128)(2,1)}, f32[8,512]{1,0:T(8,128)}, f32[128,64]{1,0:T(8,128)}, f32[24,128]{1,0:T(8,128)}) custom-call(bf16[256,64,128]{2,1,0:T(8,128)(2,1)} %pair_hbm.1, bf16[8,192]{1,0:T(8,128)(2,1)} %queries_hbm.1, bf16[8,144]{1,0:T(8,128)(2,1)} %qpoints_hbm.1, f32[8,12]{1,0:T(8,128)} %frames_hbm.1, bf16[24,64]{1,0:T(8,128)(2,1)} %bitcast.13, ...), custom_call_target="tpu_custom_call" | custom-call | tf_op jit(solution)/shard_map/main/pallas_call | solution.py:847
  64.3 5.1 %last.1 = (bf16[256,64,128]{2,1,0:T(8,128)(2,1)}, f32[8,192]{1,0:T(8,128)}, f32[8,144]{1,0:T(8,128)}, f32[24,64]{1,0:T(8,128)}, f32[18,64]{1,0:T(8,128)}, /*inde...) custom-call(bf16[256,64,128]{2,1,0:T(8,128)(2,1)} %get-tuple-element.22.pair_in, ...), custom_call_target="tpu_custom_call" | custom-call | tf_op jit(solution)/shard_map/last/pallas_call | solution.py:929

commit v2 on v1

--- a/solution.py
+++ b/solution.py
@@ -150,6 +150,33 @@
     return jnp.concatenate([tall[t * ROWS : (t + 1) * ROWS] for t in range(ROWS)], axis=1)
 
 
+def packed(vectors, points):
+    points = pltpu.roll(points, 64, 1)
+    return jnp.concatenate(
+        [vectors[:, :128], vectors[:, 128:] + points[:, :128], points[:, 128:]], axis=1
+    )
+
+
+def squared_lengths(points):
+    lane = iota((LANES, 256), 1)
+    row = whole_part(iota((LANES, 256), 0), ROWS)
+    hit = (whole_part(lane, 3 * PQ) == row) & (lane < 3.0 * H * PQ)
+    pick = jnp.where(hit, 1.0, 0.0).astype(BF16)
+    points = points.astype(BF16).astype(F32)
+    squares = points * points
+    high = squares.astype(BF16).astype(F32)
+    parts = jnp.concatenate(
+        [expanded_features(high, pick), expanded_features(squares - high, pick)], axis=1
+    )
+    total = nt(jnp.ones((ROWS, 512), BF16), parts)
+    first = total.astype(BF16).astype(F32)
+    second = (total - first).astype(BF16).astype(F32)
+    third = (total - first - second).astype(BF16).astype(F32)
+    which = iota((ROWS, LANES), 0)
+    rows = jnp.where(which == 0.0, first, jnp.where(which == 1.0, second, third))
+    return pltpu.roll(jnp.where(which < 3.0, rows, 0.0), 16, 1)
+
+
 def make_block(block, queries, qpoints, frames, gscalar, gpair, gpoints, wide, loss):
     f = frames[...]
     q = padded(wide, queries[...], 256)
@@ -158,7 +185,8 @@
     gs = padded(wide, gscalar[...], 256) * loss
     gg = rotated(f, padded(wide, gpoints[...], 384) * loss, 384, False)
     gg = pltpu.roll(gg, 64, 1)
-    tiles = [q[:, :128], q[:, 128:], qg[:, :128], qg[:, 128:], gs[:, :128]]
+    lengths = squared_lengths(qg)
+    tiles = [q[:, :128], q[:, 128:], qg[:, :128], qg[:, 128:] + lengths, gs[:, :128]]
     tiles += [gs[:, 128:] + gg[:, :128], gg[:, 128:256], gg[:, 256:]]
     pairs = gpair[...].astype(F32) * loss
     tall = [pairs[:, h * CZ : (h + 1) * CZ] for h in range(H)]
@@ -192,30 +220,29 @@
     return ((z + 8 + dz) % 8) * 4 + (y + gray(i)) % 4
 
 
-def forward_group(pairs, block, masks, mask, expanded, keys, square, masking, gamma):
-    features = wide_features(block)
-    wide = expanded_features(features, mask[...])
-    pair_side = jnp.concatenate([expanded[...], expanded_pairs(block, masks)], axis=0)
-    both = nt(pairs, pair_side)
-    bias, pair_part = both[:, :LANES], both[:, LANES:]
-    dots = nt(keys[:, 0:256], wide[:, 0:256])
-    cross = nt(keys[:, 256:512], wide[:, 256:512])
-    grads = nt(keys[:, 512:1024], wide[:, 512:1024]) + pair_part
-    points = features[:, 256:512]
-    squares = points * points
-    high = squares.astype(BF16).astype(F32)
-    pick = mask[:, 256:512]
-    parts = jnp.concatenate(
-        [expanded_features(high, pick), expanded_features(squares - high, pick)], axis=1
-    )
-    query_square = nt(jnp.ones((ROWS, 512), BF16), parts)[0:1, :]
-    distance = query_square + square[...] - 2.0 * cross
-    scores = WL * (dots * 0.25 + bias) - (DIST_WEIGHT * gamma) * distance - masking
-    top = jnp.max(scores, axis=0, keepdims=True)
-    weights = jnp.exp(scores - top)
-    total = jnp.sum(weights, axis=0, keepdims=True)
-    inner = jnp.sum(weights * grads, axis=0, keepdims=True)
-    return weights, grads, distance, top, total, inner
+def forward_groups(pairs, blocks, masks, mask, expanded, keys, square, masking, gamma):
+    rows = keys.shape[0]
+    biases = nt(jnp.concatenate(pairs, axis=0), expanded[...])
+    outs = []
+    for k, block in enumerate(blocks):
+        features = wide_features(block)
+        wide = expanded_features(features, mask[...])
+        bias = biases[k * rows : (k + 1) * rows, :]
+        dots = nt(keys[:, 0:256], wide[:, 0:256])
+        cross = nt(keys[:, 256:512], wide[:, 256:512])
+        grads = nt(keys[:, 512:1024], wide[:, 512:1024]) + nt(
+            pairs[k], expanded_pairs(block, masks)
+        )
+        line = features[0:1, 384:512] + features[1:2, 384:512] + features[2:3, 384:512]
+        query_square = pltpu.roll(line, LANES - 16, 1)
+        distance = query_square + square[...] - 2.0 * cross
+        scores = WL * (dots * 0.25 + bias) - (DIST_WEIGHT * gamma) * distance - masking
+        top = jnp.max(scores, axis=0, keepdims=True)
+        weights = jnp.exp(scores - top)
+        total = jnp.sum(weights, axis=0, keepdims=True)
+        inner = jnp.sum(weights * grads, axis=0, keepdims=True)
+        outs.append((weights, grads, distance, top, total, inner))
+    return outs
 
 
 def combine_stats(arrived, answers, table):
@@ -250,28 +277,18 @@
     return turned.astype(BF16), bias_part
 
 
-def small_group(score_half, probs_half, turned, block, mask, head_rows, keys, point_gamma):
-    features = wide_features(block)
-    wide = expanded_features(features, mask[...])
-    key_part = jnp.concatenate(
-        [nn(score_half, wide[:, 0:512]), nn(probs_half, wide[:, 512:1024])], axis=1
-    )
-    key_sum = nn(score_half, mask[:, 256:512])
-    product = nn(turned, keys[:, 0:512])
+def query_group(turned, features, head_rows, packed_keys, scale, point_scale):
+    product = nn(turned, packed_keys)
     row_sum = jnp.sum(turned.astype(F32), axis=1, keepdims=True)
-    query_part = jnp.zeros((ROWS, 512), F32)
+    query_part = jnp.zeros((ROWS, 384), F32)
     row_part = jnp.zeros((ROWS, 256), F32)
     for h in range(H):
         at = slice(h * ROWS, (h + 1) * ROWS)
-        query_part = query_part + head_rows[at, :] * product[at, :]
-        row_part = row_part + head_rows[at, 256:512] * row_sum[at, :]
-    vectors = 0.25 * query_part[:, 0:256]
-    points = (WC * point_gamma) * (query_part[:, 256:512] - features[:, 256:512] * row_part)
-    points = pltpu.roll(points, 64, 1)
-    query_out = jnp.concatenate(
-        [vectors[:, :128], vectors[:, 128:] + points[:, :128], points[:, 128:]], axis=1
-    )
-    return key_part, key_sum, query_out
+        query_part = query_part + head_rows[at, 0:384] * product[at, :]
+        row_part = row_part + head_rows[at, 384:640] * row_sum[at, :]
+    less = point_scale * pltpu.roll(features[:, 256:512], 64, 1) * row_part
+    query_part = scale * query_part
+    return jnp.concatenate([query_part[:, :128], query_part[:, 128:] - less], axis=1)
 
 
 def sum_of(ref, count):
@@ -327,6 +344,7 @@
     expanded,
     placing,
     keys,
+    packed_keys,
     square,
     weights,
     grads,
@@ -357,7 +375,8 @@
     own_sem,
     out_sem,
     send_sem,
-    recv_sem,
+    upper_recv,
+    lower_recv,
     key_send,
     key_recv,
     stats_send,
@@ -424,16 +443,21 @@
     up = (row, ((z + 1) % 8) * 4 + y)
     down = (row, ((z + 7) % 8) * 4 + y)
 
-    def send_block(source, slot, target, at):
-        remote(source, blocks.at[slot], send_sem.at[at], recv_sem.at[slot], target).start()
-
-    def block_arrived(slot):
-        remote(own_block, blocks.at[slot], send_sem.at[0], recv_sem.at[slot], here).wait_recv()
-
-    send_block(own_block, col, up, 0)
-    send_block(own_block, col, down, 1)
-    for n, d in enumerate((1, 3, 2)):
-        send_block(own_block, col, (row, z * 4 + (y + d) % 4), 2 + n)
+    parts = ((pl.ds(0, 160), upper_recv),)
+
+    def send_part(source, slot, target, part):
+        at, recv = part
+        remote(source.at[at], blocks.at[slot, at], send_sem, recv.at[slot], target).start()
+
+    def part_arrived(slot, part):
+        at, recv = part
+        remote(own_block.at[at], blocks.at[slot, at], send_sem, recv.at[slot], here).wait_recv()
+
+    for part in parts:
+        send_part(own_block, col, up, part)
+        send_part(own_block, col, down, part)
+        for d in (1, 3, 2):
+            send_part(own_block, col, (row, z * 4 + (y + d) % 4), part)
     for d in range(1, 8):
         peer = ((row + d) % 8, col)
         remote(own_piece, pieces.at[row], key_send.at[d], key_recv.at[row], peer).start()
@@ -444,7 +468,8 @@
 
     full = head_mask()
     mask[...] = full.astype(BF16)
-    head_rows[...] = full[0 : H * ROWS, 0:512]
+    head_rows[:, 0:384] = packed(full[0 : H * ROWS, 0:256], full[0 : H * ROWS, 256:512])
+    head_rows[:, 384:640] = pltpu.roll(full[0 : H * ROWS, 256:512], 64, 1)
     fill_weight(expanded, weight[...])
     fill_placing(placing)
     key_acc[...] = jnp.zeros_like(key_acc)
@@ -454,14 +479,19 @@
     masks = residue_masks()
     gamma = softplus_of(per_head(head_weight, lane_heads()))
     point_gamma = softplus_of(per_head(head_weight, feature_heads()[:, 256:512]))
+    vector_scale = jnp.where(iota((1, 256), 1) < 1.0 * H * C, 0.25, 0.0)
+    used = jnp.where(iota((1, 256), 1) < 3.0 * H * PQ, WC * point_gamma, 0.0)
+    scale = packed(vector_scale, used)
+    point_scale = pltpu.roll(used, 64, 1)
     masking = 100000.0 * (1.0 - key_mask[...].astype(F32))
     masking = jnp.broadcast_to(masking, (ROWS, masking.shape[1])).T[:, 0:1]
 
-    for n, d in enumerate((1, 3, 2)):
+    for d in (1, 3, 2):
         slot = z * 4 + (y + d) % 4
-        block_arrived(slot)
-        send_block(blocks.at[slot], slot, up, 5 + 2 * n)
-        send_block(blocks.at[slot], slot, down, 6 + 2 * n)
+        for part in parts:
+            part_arrived(slot, part)
+            send_part(blocks.at[slot], slot, up, part)
+            send_part(blocks.at[slot], slot, down, part)
     for d in range(1, 8):
         source = (row + d) % 8
         remote(own_piece, pieces.at[source], key_send.at[d], key_recv.at[source], here).wait_recv()
@@ -470,6 +500,7 @@
     tall = jnp.concatenate([pieces[r] for r in range(8)], axis=1)
     keys[...] = nn(tall, placing[...]).astype(BF16)
     points = keys[:, 256:512].astype(F32)
+    packed_keys[...] = packed(keys[:, 0:256].astype(F32), points).astype(BF16)
     squares = points * points
     high_part = squares.astype(BF16)
     low_part = (squares - high_part.astype(F32)).astype(BF16)
@@ -479,37 +510,51 @@
 
     def send_stats(slot):
         remote(
-            stats.at[slot], arrived.at[col], stats_send.at[slot], stats_recv.at[col], (row, slot)
+            stats.at[slot], arrived.at[col], stats_send, stats_recv, (row, slot)
         ).start()
 
-    def forward_one(slot):
+    def pairs_of(slot):
         first = pl.multiple_of(slot * ROWS, ROWS)
-        pairs = jnp.concatenate([pair[first + i] for i in range(ROWS)], axis=1)
-        out = forward_group(
-            pairs, blocks[slot], masks, mask, expanded, keys, square, masking, gamma
+        return [pair[first + i] for i in range(ROWS)]
+
+    def forward_two(slots):
+        pairs = [jnp.concatenate(pairs_of(slot), axis=1) for slot in slots]
+        outs = forward_groups(
+            pairs,
+            [blocks[slot] for slot in slots],
+            masks,
+            mask,
+            expanded,
+            keys,
+            square,
+            masking,
+            gamma,
         )
-        weights[slot], grads[slot], distance[slot] = out[0], out[1], out[2]
-        for n in range(3):
-            stats[slot, :, n * LANES : (n + 1) * LANES] = out[3 + n]
+        for slot, out in zip(slots, outs):
+            weights[slot], grads[slot], distance[slot] = out[0], out[1], out[2]
+            for n in range(3):
+                stats[slot, :, n * LANES : (n + 1) * LANES] = out[3 + n]
 
     def forward_step(e, _):
         low, high = ring_slots(e, z, y)
 
-        @pl.when(e >= 2)
-        def _():
-            block_arrived(low)
-
-        @pl.when((e >= 2) & (e <= 11))
-        def _():
-            send_block(blocks.at[low], low, up, 11 + e)
-
-        @pl.when(e >= 2)
-        def _():
-            block_arrived(high)
-
-        @pl.when(((e >= 2) & (e <= 9)) | ((e >= 12) & (e <= 13)))
-        def _():
-            send_block(blocks.at[high], high, down, 23 + e)
+        for part in parts:
+
+            @pl.when(e >= 2)
+            def _(part=part):
+                part_arrived(low, part)
+
+            @pl.when((e >= 2) & (e <= 11))
+            def _(part=part):
+                send_part(blocks.at[low], low, up, part)
+
+            @pl.when(e >= 2)
+            def _(part=part):
+                part_arrived(high, part)
+
+            @pl.when(((e >= 2) & (e <= 9)) | ((e >= 12) & (e <= 13)))
+            def _(part=part):
+                send_part(blocks.at[high], high, down, part)
 
         @pl.when(e >= 1)
         def _():
@@ -519,8 +564,7 @@
         def _():
             send_stats(ring_slots(e - 1, z, y)[1])
 
-        forward_one(low)
-        forward_one(high)
+        forward_two((low, high))
         return 0
 
     lax.fori_loop(0, 16, forward_step, 0)
@@ -528,14 +572,12 @@
     for slot in ring_slots(15, z, y):
         send_stats(slot)
 
-    def stats_arrived(d, _):
-        peer = (col + d) % 32
-        remote(
-            stats.at[peer], arrived.at[peer], stats_send.at[peer], stats_recv.at[peer], here
-        ).wait_recv()
-        return 0
-
-    lax.fori_loop(1, 32, stats_arrived, 0)
+    most = pl.ds(0, groups - 1)
+
+    def all_of(buffer, sem):
+        pltpu.make_async_copy(buffer.at[most], buffer.at[most], sem).wait()
+
+    all_of(arrived, stats_recv)
     combine_stats(arrived, answers, table)
 
     for d in range(16, 48):
@@ -544,15 +586,14 @@
             remote(
                 answers.at[peer],
                 answered.at[col],
-                answer_send.at[peer],
+                answer_send,
                 answer_recv.at[col],
                 (row, peer),
             ).start()
     answered[col] = answers[col]
 
     def score_one(slot, k):
-        first = pl.multiple_of(slot * ROWS, ROWS)
-        pairs = [pair[first + i] for i in range(ROWS)]
+        pairs = pairs_of(slot)
         score_half, probs_half, head_part = score_group(
             answered[slot, :, 0:LANES],
             answered[slot, :, LANES : 2 * LANES],
@@ -567,7 +608,7 @@
 
     def answer_arrived(slot):
         remote(
-            answers.at[slot], answered.at[slot], answer_send.at[slot], answer_recv.at[slot], here
+            answers.at[slot], answered.at[slot], answer_send, answer_recv.at[slot], here
         ).wait_recv()
 
     def score_step(e, _):
@@ -585,8 +626,8 @@
         return 0
 
     lax.fori_loop(0, 16, score_step, 0)
-    totals[0, 0:16, :] = bias_acc[...]
-    totals[0, 16:24, :] = jnp.broadcast_to(head_acc[...], (ROWS, LANES))
+    totals[0, :, :] = bias_acc[...]
+    totals[0, H : H + 1, :] = head_acc[...]
 
     def spread_total(source, target, me, count, base, device):
         for d in range(1, count):
@@ -610,22 +651,23 @@
 
     def send_query(slot):
         remote(
-            query_parts.at[slot], query_in.at[col], query_send.at[slot], query_recv.at[col], (row, slot)
+            query_parts.at[slot], query_in.at[col], query_send, query_recv, (row, slot)
         ).start()
 
-    def small_one(slot):
-        out = small_group(
-            halves[slot, :, 0:LANES],
-            halves[slot, :, LANES : 2 * LANES],
-            turned[slot],
-            blocks[slot],
-            mask,
-            head_rows,
-            keys,
-            point_gamma,
-        )
-        query_parts[slot] = out[2].astype(BF16)
-        return out[0], out[1]
+    def small_two(slots):
+        wides = []
+        for slot in slots:
+            features = wide_features(blocks[slot])
+            wides.append(expanded_features(features, mask[...]))
+            query_parts[slot] = query_group(
+                turned[slot], features, head_rows, packed_keys[...], scale, point_scale
+            ).astype(BF16)
+        wide = jnp.concatenate(wides, axis=0)
+        scores = [halves[slot, :, 0:LANES] for slot in slots]
+        probs = [halves[slot, :, LANES : 2 * LANES] for slot in slots]
+        key_acc[:, 0:512] += nn(jnp.concatenate(scores, axis=1), wide[:, 0:512])
+        key_acc[:, 512:1024] += nn(jnp.concatenate(probs, axis=1), wide[:, 512:1024])
+        sum_acc[...] += scores[0].astype(F32) + scores[1].astype(F32)
 
     def small_step(e, _):
         first, second = near_slot(31 - 2 * e, z, y), near_slot(30 - 2 * e, z, y)
@@ -635,15 +677,12 @@
             send_query(near_slot(33 - 2 * e, z, y))
             send_query(near_slot(32 - 2 * e, z, y))
 
-        key_a, sum_a = small_one(first)
-        key_b, sum_b = small_one(second)
-        key_acc[...] += key_a + key_b
-        sum_acc[...] += sum_a + sum_b
+        small_two((first, second))
         return 0
 
     def stage_copy(slot):
         at = pl.ds(pl.multiple_of(slot * ROWS, ROWS), ROWS)
-        return pltpu.make_async_copy(pair_stage.at[at], pair_out.at[at], out_sem.at[slot])
+        return pltpu.make_async_copy(pair_stage.at[at], pair_out.at[at], out_sem)
 
     def pair_step(e, _):
         @pl.when(e >= 1)
@@ -673,8 +712,11 @@
     totals[2] = sum_of(y_in, 4)
     z_in[z] = totals[2]
     spread_total(totals.at[2], z_in, z, 8, 12, lambda p: (row, p * 4 + y))
+    sum_high = sum_acc[...].astype(BF16)
+    sum_low = (sum_acc[...] - sum_high.astype(F32)).astype(BF16)
+    key_sum = nn(sum_high, mask[:, 256:512]) + nn(sum_low, mask[:, 256:512])
     key_points = (WC * point_gamma) * (
-        key_acc[:, 256:512] - keys[:, 256:512].astype(F32) * sum_acc[...]
+        key_acc[:, 256:512] - keys[:, 256:512].astype(F32) * key_sum
     )
     whole = jnp.concatenate(
         [0.25 * key_acc[:, 0:256], key_points, key_acc[:, 512:1024]], axis=1
@@ -691,14 +733,7 @@
 
     lax.fori_loop(2, 16, pair_step, 0)
 
-    def query_arrived(d, _):
-        peer = (col + d) % 32
-        remote(
-            query_parts.at[peer], query_in.at[peer], query_send.at[peer], query_recv.at[peer], here
-        ).wait_recv()
-        return 0
-
-    lax.fori_loop(1, 32, query_arrived, 0)
+    all_of(query_in, query_recv)
     mine = sum_of(query_in, 32)
     query_out[:, 0:256] = mine[:, 0:256]
     back = pltpu.roll(mine, 384 - 192, 1)[:, 0:256]
@@ -716,37 +751,21 @@
     total_arrived(totals.at[2], z_in, z, 8, 12)
     total_out[...] = sum_of(z_in, 8)
 
-    for at in list(range(11)) + list(range(13, 23)) + list(range(25, 33)) + [35, 36]:
-        remote(own_block, blocks.at[0], send_sem.at[at], recv_sem.at[0], here).wait_send()
+    all_of(blocks, send_sem)
     for d in range(1, 8):
         remote(own_piece, pieces.at[0], key_send.at[d], key_recv.at[0], here).wait_send()
         remote(key_parts.at[0], key_in.at[0], part_send.at[d], part_recv.at[0], here).wait_send()
 
-    def all_left(d, _):
-        peer = (col + d) % 32
-        remote(
-            stats.at[peer], arrived.at[peer], stats_send.at[peer], stats_recv.at[peer], here
-        ).wait_send()
-        remote(
-            answers.at[peer], answered.at[peer], answer_send.at[peer], answer_recv.at[peer], here
-        ).wait_send()
-        remote(
-            query_parts.at[peer], query_in.at[peer], query_send.at[peer], query_recv.at[peer], here
-        ).wait_send()
-        return 0
-
-    lax.fori_loop(1, 32, all_left, 0)
+    all_of(arrived, stats_send)
+    all_of(answers, answer_send)
+    all_of(query_in, query_send)
     for base, count in ((0, 8), (8, 4), (12, 8)):
         for d in range(1, count):
             remote(
                 totals.at[0], row_in.at[0], total_send.at[base + d], total_recv.at[0], here
             ).wait_send()
 
-    def stage_left(slot, _):
-        stage_copy(slot).wait()
-        return 0
-
-    lax.fori_loop(0, groups, stage_left, 0)
+    pltpu.make_async_copy(pair_stage, pair_out, out_sem).wait()
 
 
 def last_kernel(
@@ -786,7 +805,7 @@
     bias_grad[...] = total_sum[0:H, :] * (1.0 / residues)
     heads = lane_heads()
     raw = per_head(head_weight, heads)
-    line = total_sum[16:17, :] * (-DIST_WEIGHT / residues) / (1.0 + jnp.exp(-raw))
+    line = total_sum[H : H + 1, :] * (-DIST_WEIGHT / residues) / (1.0 + jnp.exp(-raw))
     for h in range(H):
         head_grad[h] = jnp.sum(jnp.where(heads == float(h), line, 0.0))
     for k in range(pieces):
@@ -850,7 +869,7 @@
             shape(rows, keys, LANES, dtype=BF16),
             shape(ROWS, 512),
             shape(LANES, keys),
-            shape(24, LANES),
+            shape(16, LANES),
         ),
         in_specs=[HBM] * (1 + len(given)),
         out_specs=(HBM, VMEM, VMEM, VMEM),
@@ -864,10 +883,11 @@
             full((LANES, keys), F32),
             full((ROWS, 384), F32),
             half(LANES, FEATURES),
-            full((H * ROWS, 512), F32),
+            full((H * ROWS, 640), F32),
             half(LANES, FEATURES),
             half(FEATURES, FEATURES),
             half(keys, FEATURES),
+            half(keys, 384),
             full((keys, LANES), F32),
             full((groups, keys, LANES), F32),
             full((groups, keys, LANES), F32),
@@ -882,31 +902,32 @@
             half(groups, LANES, keys),
             full((2, LANES, keys), F32),
             full((keys, FEATURES), F32),
-            full((keys, 256), F32),
+            full((keys, LANES), F32),
             full((16, LANES), F32),
             full((1, LANES), F32),
             half(groups, ROWS, 384),
             half(groups, ROWS, 384),
             half(8, keys, LANES),
             half(8, keys, LANES),
-            full((3, 24, LANES), F32),
-            full((8, 24, LANES), F32),
-            full((4, 24, LANES), F32),
-            full((8, 24, LANES), F32),
+            full((3, 16, LANES), F32),
+            full((8, 16, LANES), F32),
+            full((4, 16, LANES), F32),
+            full((8, 16, LANES), F32),
             DMA((len(given),)),
             DMA((4,)),
             DMA((2,)),
+            DMA,
+            DMA,
             DMA((groups,)),
-            DMA((40,)),
-            DMA((32,)),
+            DMA((groups,)),
             DMA((8,)),
             DMA((8,)),
-            DMA((32,)),
-            DMA((32,)),
-            DMA((32,)),
-            DMA((32,)),
-            DMA((32,)),
-            DMA((32,)),
+            DMA,
+            DMA,
+            DMA,
+            DMA((groups,)),
+            DMA,
+            DMA,
             DMA((8,)),
             DMA((8,)),
             DMA((20,)),

time: 69.6 us -> 66.1 us (0.950)
  Pallas kernels: 68.7 us -> 65.2 us
    pallas_call x1, Pallas kernels: 63.6 us -> 60.1 us  [local(): pl.pallas_call(functools.partial(main_kernel, loss, float(residues)), out...]
where the time goes in v2:
time: 66.1 us; the launch traced here: 65.9 us
  Pallas kernels  65.2 us (99%)
    pallas_call x1, Pallas kernels, local(): pl.pallas_call(functools.partial(main_kernel, loss, float(residues)), out...  60.1 us
    pallas_call x1, Pallas kernels, local(): pl.pallas_call(functools.partial(last_kernel, float(residues)), out_shape...  5.1 us

profile of v2, /device:TPU:1, one launch (start us, length us, event | category | flops | bytes accessed | tf_op | source)
XLA Modules:
  0.0 65.9 jit_solution(13728211531855564143)
XLA Ops:
  0.6 60.1 %main.1 = (bf16[256,64,128]{2,1,0:T(8,128)(2,1)}, f32[8,512]{1,0:T(8,128)}, f32[128,64]{1,0:T(8,128)}, f32[16,128]{1,0:T(8,128)}) custom-call(bf16[256,64,128]{2,1,0:T(8,128)(2,1)} %pair_hbm.1, bf16[8,192]{1,0:T(8,128)(2,1)} %queries_hbm.1, bf16[8,144]{1,0:T(8,128)(2,1)} %qpoints_hbm.1, f32[8,12]{1,0:T(8,128)} %frames_hbm.1, bf16[24,64]{1,0:T(8,128)(2,1)} %bitcast.13, ...), custom_call_target="tpu_custom_call" | custom-call | tf_op jit(solution)/shard_map/main/pallas_call | solution.py:866
  60.8 5.1 %last.1 = (bf16[256,64,128]{2,1,0:T(8,128)(2,1)}, f32[8,192]{1,0:T(8,128)}, f32[8,144]{1,0:T(8,128)}, f32[24,64]{1,0:T(8,128)}, f32[18,64]{1,0:T(8,128)}, /*inde...) custom-call(bf16[256,64,128]{2,1,0:T(8,128)(2,1)} %get-tuple-element.22.pair_in, ...), custom_call_target="tpu_custom_call" | custom-call | tf_op jit(solution)/shard_map/last/pallas_call | solution.py:950

commit v3 on v2

--- a/solution.py
+++ b/solution.py
@@ -316,9 +316,9 @@
     gpair_hbm,
     gpoints_hbm,
     pair_out,
-    query_out,
-    key_out,
-    total_out,
+    query_hbm,
+    key_hbm,
+    total_hbm,
     queries,
     qpoints,
     frames,
@@ -355,6 +355,9 @@
     answered,
     table,
     halves,
+    query_out,
+    key_out,
+    total_out,
     pair_stage,
     turned,
     flipped,
@@ -370,6 +373,7 @@
     row_in,
     y_in,
     z_in,
+    small_sem,
     input_sem,
     pair_sem,
     own_sem,
@@ -612,20 +616,20 @@
         ).wait_recv()
 
     def score_step(e, _):
-        first, second = near_slot(2 * e, z, y), near_slot(2 * e + 1, z, y)
+        slots = [near_slot(4 * e + k, z, y) for k in range(4)]
 
         @pl.when(e >= 1)
         def _():
-            answer_arrived(first)
-
-        answer_arrived(second)
-        bias_a, head_a = score_one(first, 0)
-        bias_b, head_b = score_one(second, 1)
-        bias_acc[...] += bias_a + bias_b
-        head_acc[...] += head_a + head_b
+            answer_arrived(slots[0])
+
+        for slot in slots[1:]:
+            answer_arrived(slot)
+        parts = [score_one(slot, k) for k, slot in enumerate(slots)]
+        bias_acc[...] += (parts[0][0] + parts[1][0]) + (parts[2][0] + parts[3][0])
+        head_acc[...] += (parts[0][1] + parts[1][1]) + (parts[2][1] + parts[3][1])
         return 0
 
-    lax.fori_loop(0, 16, score_step, 0)
+    lax.fori_loop(0, 8, score_step, 0)
     totals[0, :, :] = bias_acc[...]
     totals[0, H : H + 1, :] = head_acc[...]
 
@@ -740,15 +744,22 @@
     lane = iota((ROWS, 256), 1)
     back = jnp.where(lane < 3.0 * H * PQ, back, 0.0)
     query_out[:, 256:512] = rotated(frames[...], back, 256, True)
+    stage_copy(groups - 2).start()
+    stage_copy(groups - 1).start()
     for d in range(1, 8):
         peer = (row + d) % 8
         remote(
             key_parts.at[peer], key_in.at[peer], part_send.at[d], part_recv.at[peer], here
         ).wait_recv()
     key_out[...] = sum_of(key_in, 8).T
-    stage_copy(groups - 2).start()
-    stage_copy(groups - 1).start()
+    small_copies = [
+        pltpu.make_async_copy(query_out, query_hbm, small_sem.at[0]),
+        pltpu.make_async_copy(key_out, key_hbm, small_sem.at[1]),
+        pltpu.make_async_copy(total_out, total_hbm, small_sem.at[2]),
+    ]
+    small_copies[0].start()
     total_arrived(totals.at[2], z_in, z, 8, 12)
+    small_copies[1].start()
     total_out[...] = sum_of(z_in, 8)
 
     all_of(blocks, send_sem)
@@ -765,54 +776,65 @@
                 totals.at[0], row_in.at[0], total_send.at[base + d], total_recv.at[0], here
             ).wait_send()
 
+    small_copies[2].start()
     pltpu.make_async_copy(pair_stage, pair_out, out_sem).wait()
-
-
-def last_kernel(
-    residues,
-    pair_in,
-    head_weight,
-    query_sum,
-    key_sum,
-    total_sum,
-    pair_grad,
-    queries_grad,
-    qpoints_grad,
-    keyset_grad,
-    kpoints_grad,
-    values_grad,
-    vpoints_grad,
-    bias_grad,
-    head_grad,
-    stage,
-    in_sem,
-    out_sem,
-):
+    for copy in small_copies:
+        copy.wait()
+
+
+def last_kernel(residues, *refs):
+    pair_in, head_hbm, query_hbm, key_hbm, total_hbm = refs[:5]
+    pair_grad, *outs = refs[5:14]
+    stage, head_weight, query_sum, key_sum, total_sum, *finals = refs[14:27]
+    in_sem, out_sem, small_in, small_out = refs[27:]
     pieces = in_sem.shape[0]
     size = stage.shape[0] // pieces
     arrivals, leaves = [], []
+    smalls = (
+        (head_hbm, head_weight),
+        (query_hbm, query_sum),
+        (key_hbm, key_sum),
+        (total_hbm, total_sum),
+    )
+    small_copies = [
+        pltpu.make_async_copy(source, target, small_in.at[k])
+        for k, (source, target) in enumerate(smalls)
+    ]
     for k in range(pieces):
         at = pl.ds(k * size, size)
         arrivals.append(pltpu.make_async_copy(pair_in.at[at], stage.at[at], in_sem.at[k]))
         leaves.append(pltpu.make_async_copy(stage.at[at], pair_grad.at[at], out_sem.at[k]))
         arrivals[k].start()
+        if k < len(small_copies):
+            small_copies[k].start()
+    for copy in small_copies:
+        copy.wait()
+    queries_grad, qpoints_grad, *turned, bias_grad, head_grad = finals
     queries_grad[...] = query_sum[:, 0:192]
     qpoints_grad[...] = query_sum[:, 256:400]
     at = 0
-    for out in (keyset_grad, kpoints_grad, values_grad, vpoints_grad):
+    for out in turned:
         out[...] = key_sum[at : at + out.shape[0], :]
         at += out.shape[0]
     bias_grad[...] = total_sum[0:H, :] * (1.0 / residues)
     heads = lane_heads()
     raw = per_head(head_weight, heads)
     line = total_sum[H : H + 1, :] * (-DIST_WEIGHT / residues) / (1.0 + jnp.exp(-raw))
+    lane = iota((1, LANES), 1)
+    total = jnp.zeros((1, LANES), F32)
     for h in range(H):
-        head_grad[h] = jnp.sum(jnp.where(heads == float(h), line, 0.0))
+        part = jnp.sum(jnp.where(heads == float(h), line, 0.0), axis=1, keepdims=True)
+        total = jnp.where(lane == float(h), part, total)
+    head_grad[...] = total[:, 0:H]
     for k in range(pieces):
         arrivals[k].wait()
         leaves[k].start()
-    for k in range(pieces):
-        leaves[k].wait()
+    for k, (source, target) in enumerate(zip(finals, outs)):
+        copy = pltpu.make_async_copy(source, target, small_out.at[k])
+        copy.start()
+        leaves.append(copy)
+    for copy in leaves:
+        copy.wait()
 
 
 def shape(*dims, dtype=F32):
@@ -872,7 +894,7 @@
             shape(16, LANES),
         ),
         in_specs=[HBM] * (1 + len(given)),
-        out_specs=(HBM, VMEM, VMEM, VMEM),
+        out_specs=(HBM,) * 4,
         scratch_shapes=[
             *(full(array.shape, array.dtype) for array in given),
             half(rows, keys, LANES),
@@ -898,9 +920,12 @@
             full((groups, 1, 2 * LANES), F32),
             full((3, groups, LANES), F32),
             half(groups, keys, 2 * LANES),
+            full((ROWS, 512), F32),
+            full((LANES, keys), F32),
+            full((16, LANES), F32),
             half(rows, keys, LANES),
             half(groups, LANES, keys),
-            full((2, LANES, keys), F32),
+            full((4, LANES, keys), F32),
             full((keys, FEATURES), F32),
             full((keys, LANES), F32),
             full((16, LANES), F32),
@@ -913,6 +938,7 @@
             full((8, 16, LANES), F32),
             full((4, 16, LANES), F32),
             full((8, 16, LANES), F32),
+            DMA((3,)),
             DMA((len(given),)),
             DMA((4,)),
             DMA((2,)),
@@ -946,17 +972,28 @@
         (24, keys),
         (36, keys),
         (H, CZ),
+        (1, H),
     )
     pair_grad, queries_grad, qpoints_grad, *turned, bias_grad, head_grad = pl.pallas_call(
         functools.partial(last_kernel, float(residues)),
         out_shape=(
             shape(rows, keys, LANES, dtype=BF16),
             *(shape(*dims) for dims in finals),
-            shape(H),
         ),
-        in_specs=[HBM] + [VMEM] * 4,
-        out_specs=(HBM,) + (VMEM,) * 7 + (SMEM,),
-        scratch_shapes=[half(rows, keys, LANES), DMA((8,)), DMA((8,))],
+        in_specs=[HBM] * 5,
+        out_specs=(HBM,) * 9,
+        scratch_shapes=[
+            half(rows, keys, LANES),
+            full((1, H), F32),
+            full((ROWS, 512), F32),
+            full((LANES, keys), F32),
+            full((16, LANES), F32),
+            *(full(dims, F32) for dims in finals),
+            DMA((8,)),
+            DMA((8,)),
+            DMA((4,)),
+            DMA((8,)),
+        ],
         compiler_params=pltpu.CompilerParams(vmem_limit_bytes=67043328),
         name="last",
     )(pair_main, head_weight.reshape(1, H), query_sum, key_sum, total_sum)
@@ -966,7 +1003,7 @@
         qpoints_grad,
         *(array.T for array in turned),
         bias_grad.T,
-        head_grad,
+        head_grad.reshape(H),
     )
 
 

time: 66.1 us -> 63.7 us (0.964)
  Pallas kernels: 65.2 us -> 62.9 us
    pallas_call x1, Pallas kernels: 60.1 us -> 58.6 us  [local(): pl.pallas_call(functools.partial(main_kernel, loss, float(residues)), out...]
    pallas_call x1, Pallas kernels: 5.1 us -> 4.34 us  [local(): pl.pallas_call(functools.partial(last_kernel, float(residues)), out_shape...]
where the time goes in v3:
time: 63.7 us; the launch traced here: 63.6 us
  Pallas kernels  62.9 us (99%)
  between operations  0.66 us (1%)
    pallas_call x1, Pallas kernels, local(): pl.pallas_call(functools.partial(main_kernel, loss, float(residues)), out...  58.6 us
    pallas_call x1, Pallas kernels, local(): pl.pallas_call(functools.partial(last_kernel, float(residues)), out_shape...  4.34 us

profile of v3, /device:TPU:1, one launch (start us, length us, event | category | flops | bytes accessed | tf_op | source)
XLA Modules:
  0.0 63.6 jit_solution(14339196470572085508)
XLA Ops:
  0.6 58.6 %main.1 = (bf16[256,64,128]{2,1,0:T(8,128)(2,1)}, f32[8,512]{1,0:T(8,128)}, f32[128,64]{1,0:T(8,128)}, f32[16,128]{1,0:T(8,128)}) custom-call(bf16[256,64,128]{2,1,0:T(8,128)(2,1)} %pair_hbm.1, bf16[8,192]{1,0:T(8,128)(2,1)} %queries_hbm.1, bf16[8,144]{1,0:T(8,128)(2,1)} %qpoints_hbm.1, f32[8,12]{1,0:T(8,128)} %frames_hbm.1, bf16[24,64]{1,0:T(8,128)(2,1)} %bitcast.14, ...), custom_call_target="tpu_custom_call" | custom-call | tf_op jit(solution)/shard_map/main/pallas_call | solution.py:888
  59.2 4.3 %last.1 = (bf16[256,64,128]{2,1,0:T(8,128)(2,1)}, f32[8,192]{1,0:T(8,128)}, f32[8,144]{1,0:T(8,128)}, f32[24,64]{1,0:T(8,128)}, f32[18,64]{1,0:T(8,128)}, /*inde...) custom-call(bf16[256,64,128]{2,1,0:T(8,128)(2,1)} %get-tuple-element.22.refs_0_, ...), custom_call_target="tpu_custom_call" | custom-call | tf_op jit(solution)/shard_map/last/pallas_call | solution.py:977
